TPU v7x, 32 devices: a whole 2x2x4 slice. The times are simulated.
32 devices in a mesh: dp: 8 (over y, x, core), tensor: 4 (over z).
Axes of the slice: x: 2, y: 2, z: 4, core: 2. Of those that a mesh axis runs over, the one named last changes fastest.
Arguments:
- tokens: bfloat16 [12288, 768], P('dp'), may hold values from -6 to 6
- lengths: int32 [8, 3], P('dp'), may hold values from 1 to 1024, 1536 in all within a row
- deal_order: int32 [12288], P('dp'), may hold values from 0 to 12287, as said below
- w_qkv: float32 [3, 768, 768], P(None, None, 'tensor'), may hold values from -0.21875 to 0.21875
- b_qv: float32 [2, 768], P(None, 'tensor'), may hold values from -3 to 3
- w_out: float32 [768, 768], P('tensor'), may hold values from -2.5 to 2.5
- b_out: float32 [768], replicated, may hold values from -2 to 2
- ln1_gain: float32 [768], replicated, may hold values from 0.5 to 1.5
- ln1_bias: float32 [768], replicated, may hold values from -2 to 2
- w_up: float32 [768, 3072], P(None, 'tensor'), may hold values from -0.21875 to 0.21875
- b_up: float32 [3072], P('tensor'), may hold values from -3 to 3
- w_down: float32 [3072, 768], P('tensor'), may hold values from -0.109375 to 0.109375
- b_down: float32 [768], replicated, may hold values from -2 to 2
- ln2_gain: float32 [768], replicated, may hold values from 0.5 to 1.5
- ln2_bias: float32 [768], replicated, may hold values from -2 to 2
- cotangent: bfloat16 [12288, 768], P('dp'), may hold values from -6 to 6
Outputs:
- output: bfloat16 [12288, 768], P('dp')
- input_grad: bfloat16 [12288, 768], P('dp')
- grad_w_qkv: float32 [3, 768, 768], P(None, None, 'tensor')
- grad_b_qv: float32 [2, 768], P(None, 'tensor')
- grad_w_out: float32 [768, 768], P('tensor')
- grad_b_out: float32 [768], replicated
- grad_ln1_gain: float32 [768], replicated
- grad_ln1_bias: float32 [768], replicated
- grad_w_up: float32 [768, 3072], P(None, 'tensor')
- grad_b_up: float32 [3072], P('tensor')
- grad_w_down: float32 [3072, 768], P('tensor')
- grad_b_down: float32 [768], replicated
- grad_ln2_gain: float32 [768], replicated
- grad_ln2_bias: float32 [768], replicated
Inputs may be any that keep to these rules, and one draw needn't show every extreme that they name: deal_order is a permutation of 0 to 12287. With b = 192, the token in row t of the s-th block of 1536 rows goes to a position p with (p mod 1536) // b equal to s. Each row of lengths sums to 1536.
All inputs are finite; a program needn't handle non-finite values.
Results may differ from a plain program's by a relative error of at most 0.02.
Values may be sent and summed in bfloat16 or wider, within the bound.
A program may use at most 128 MiB of HBM per device.

v0:
```python
import math
import jax
import jax.numpy as jnp
from jax import lax
from jax.sharding import PartitionSpec as P

HD = 64


def layer_norm(summed, gain_vec, bias_vec):
    average = jnp.mean(summed, axis=-1, keepdims=True)
    centered = summed - average
    variance = jnp.mean(centered * centered, axis=-1, keepdims=True)
    return centered * lax.rsqrt(variance + 1e-06) * gain_vec + bias_vec


def exact_gelu(values):
    return jax.nn.gelu(values, approximate=False)


def own_slice(rows, groups, pieces, part_index):
    width = rows.shape[1]
    sub_len = rows.shape[0] // (groups * pieces)
    shaped = rows.reshape(groups, pieces, sub_len, width)
    picked = lax.dynamic_slice_in_dim(shaped, part_index, 1, 1)
    return picked.reshape(groups * sub_len, width)


def to_owned(rows, groups, pieces):
    width = rows.shape[1]
    sub_len = rows.shape[0] // (groups * pieces)
    return rows.reshape(groups, pieces, sub_len, width).swapaxes(0, 1).reshape(rows.shape[0], width)


def from_owned(rows, groups, pieces):
    width = rows.shape[1]
    sub_len = rows.shape[0] // (groups * pieces)
    return rows.reshape(pieces, groups, sub_len, width).swapaxes(0, 1).reshape(rows.shape[0], width)


def on_device(
    tokens,
    lengths,
    deal_order,
    w_qkv,
    b_qv,
    w_out,
    b_out,
    ln1_gain,
    ln1_bias,
    w_up,
    b_up,
    w_down,
    b_down,
    ln2_gain,
    ln2_bias,
    cotangent,
):
    groups = lax.axis_size("dp")
    pieces = lax.axis_size("tensor")
    part_index = lax.axis_index("tensor")
    tok_count = tokens.shape[0]
    block_len = tok_count // groups
    sub_len = block_len // pieces
    local_heads = w_qkv.shape[2] // HD
    query_scale = HD ** (-0.5)
    slot_index = deal_order // tok_count * block_len + deal_order % block_len
    send_tokens = jnp.zeros_like(tokens).at[slot_index].set(tokens)
    send_cot = jnp.zeros_like(cotangent).at[slot_index].set(cotangent)
    got_tokens, got_cot = (
        lax.all_to_all(send_tokens, "dp", split_axis=0, concat_axis=0, tiled=True),
        lax.all_to_all(send_cot, "dp", split_axis=0, concat_axis=0, tiled=True),
    )
    dealt_owned = to_owned(got_tokens, groups, pieces)
    own_tokens = own_slice(got_tokens, groups, pieces, part_index)
    own_cot = own_slice(got_cot, groups, pieces, part_index)
    positions = jnp.arange(tok_count, dtype=jnp.int32)
    seq_ends = jnp.cumsum(lengths[0], dtype=jnp.int32)
    segment_id = jnp.sum((positions[:, None] >= seq_ends[None, :]).astype(jnp.int32), axis=1)
    wqkv_low = w_qkv.astype(jnp.bfloat16)
    bias_qv = b_qv.astype(jnp.bfloat16).astype(jnp.float32)
    wout_low = w_out.astype(jnp.bfloat16)
    bias_out = b_out.astype(jnp.bfloat16).astype(jnp.float32)
    wup_low = w_up.astype(jnp.bfloat16)
    bup_low = b_up.astype(jnp.bfloat16)
    wdown_low = w_down.astype(jnp.bfloat16)
    bias_down = b_down.astype(jnp.bfloat16).astype(jnp.float32)
    projected = jnp.einsum("td,cde->cte", got_tokens, wqkv_low, preferred_element_type=jnp.float32)
    query_low = (
        ((projected[0] + bias_qv[0]) * query_scale)
        .astype(jnp.bfloat16)
        .reshape(tok_count, local_heads, HD)
    )
    key_low = projected[1].astype(jnp.bfloat16).reshape(tok_count, local_heads, HD)
    value_low = (projected[2] + bias_qv[1]).astype(jnp.bfloat16).reshape(tok_count, local_heads, HD)
    row_block = math.gcd(512, tok_count)
    block_count = tok_count // row_block

    def block_scores(first_row):
        query_part = lax.dynamic_slice_in_dim(query_low, first_row, row_block, 0)
        segment_part = lax.dynamic_slice_in_dim(segment_id, first_row, row_block, 0)
        scores = jnp.einsum("qhd,khd->hqk", query_part, key_low, preferred_element_type=jnp.float32)
        same_doc = segment_part[:, None] == segment_id[None, :]
        return (query_part, jnp.where(same_doc[None], scores, -1000000000.0))

    def attend(block_index):
        query_part, scores = block_scores(block_index * row_block)
        row_max = jnp.max(scores, axis=-1, keepdims=True)
        exp_scores = jnp.exp(scores - row_max)
        row_total = jnp.sum(exp_scores, axis=-1, keepdims=True)
        probs_low = (exp_scores / row_total).astype(jnp.bfloat16)
        block_out = jnp.einsum(
            "hqk,khd->qhd", probs_low, value_low, preferred_element_type=jnp.float32
        )
        return (block_out.astype(jnp.bfloat16), row_max[..., 0] + jnp.log(row_total[..., 0]))

    attended_blocks, log_totals = lax.map(attend, jnp.arange(block_count, dtype=jnp.int32))
    attended = attended_blocks.reshape(tok_count, local_heads * HD)
    attended_owned = to_owned(attended, groups, pieces)
    picked = attended_owned
    attn_part = lax.psum_scatter(
        jnp.dot(picked, wout_low, preferred_element_type=jnp.float32),
        "tensor",
        scatter_dimension=0,
        tiled=True,
    )
    sum_first = attn_part + bias_out + own_tokens.astype(jnp.float32)
    hidden, first_back = jax.vjp(layer_norm, sum_first, ln1_gain, ln1_bias)
    hidden_low = hidden.astype(jnp.bfloat16)
    hidden_all = lax.all_gather(hidden_low, "tensor", axis=0, tiled=True)
    up_input = jnp.dot(hidden_all, wup_low, preferred_element_type=jnp.float32) + bup_low.astype(
        jnp.float32
    )
    activated, gelu_back = jax.vjp(exact_gelu, up_input)
    activated_low = activated.astype(jnp.bfloat16)
    picked = activated_low
    ffn_part = lax.psum_scatter(
        jnp.dot(picked, wdown_low, preferred_element_type=jnp.float32),
        "tensor",
        scatter_dimension=0,
        tiled=True,
    )
    sum_second = ffn_part + bias_down + hidden
    result, second_back = jax.vjp(layer_norm, sum_second, ln2_gain, ln2_bias)
    g_second, grad_ln2_gain, grad_ln2_bias = second_back(own_cot.astype(jnp.float32))
    grad_b_down = jnp.sum(g_second, axis=0)
    g_ffn_low = g_second.astype(jnp.bfloat16)
    g_ffn_all = lax.all_gather(g_ffn_low, "tensor", axis=0, tiled=True)
    (g_activated,) = gelu_back(jnp.dot(g_ffn_all, wdown_low.T, preferred_element_type=jnp.float32))
    g_up_low = g_activated.astype(jnp.bfloat16)
    grad_w_down = jnp.dot(activated_low.T, g_ffn_all, preferred_element_type=jnp.float32)
    grad_w_up = jnp.dot(hidden_all.T, g_up_low, preferred_element_type=jnp.float32)
    grad_b_up = jnp.sum(g_up_low.astype(jnp.float32), axis=0)
    picked = g_up_low
    g_hidden_ffn = lax.psum_scatter(
        jnp.dot(picked, wup_low.T, preferred_element_type=jnp.float32),
        "tensor",
        scatter_dimension=0,
        tiled=True,
    )
    g_hidden = g_second + g_hidden_ffn
    g_first, grad_ln1_gain, grad_ln1_bias = first_back(g_hidden)
    grad_b_out = jnp.sum(g_first, axis=0)
    g_attn_owned = lax.all_gather(g_first.astype(jnp.bfloat16), "tensor", axis=0, tiled=True)
    grad_w_out = jnp.dot(attended_owned.T, g_attn_owned, preferred_element_type=jnp.float32)
    g_attn_all = from_owned(g_attn_owned, groups, pieces)
    g_attended = (
        jnp.dot(g_attn_all, wout_low.T, preferred_element_type=jnp.float32)
        .astype(jnp.bfloat16)
        .reshape(tok_count, local_heads, HD)
    )

    def attend_back(carry, block_data):
        grad_key, grad_value = carry
        block_index, log_total = block_data
        first_row = block_index * row_block
        query_part, scores = block_scores(first_row)
        probs = jnp.exp(scores - log_total[..., None])
        probs_low = probs.astype(jnp.bfloat16)
        upstream = lax.dynamic_slice_in_dim(g_attended, first_row, row_block, 0)
        g_probs = jnp.einsum(
            "qhd,khd->hqk", upstream, value_low, preferred_element_type=jnp.float32
        )
        inner = jnp.sum(probs * g_probs, axis=-1, keepdims=True)
        g_scores = (probs * (g_probs - inner)).astype(jnp.bfloat16)
        g_query = jnp.einsum(
            "hqk,khd->qhd", g_scores, key_low, preferred_element_type=jnp.float32
        ).astype(jnp.bfloat16)
        grad_key = grad_key + jnp.einsum(
            "hqk,qhd->khd", g_scores, query_part, preferred_element_type=jnp.float32
        )
        grad_value = grad_value + jnp.einsum(
            "hqk,qhd->khd", probs_low, upstream, preferred_element_type=jnp.float32
        )
        return ((grad_key, grad_value), g_query)

    zero_state = jnp.zeros((tok_count, local_heads, HD), jnp.float32)
    (grad_key, grad_value), g_query_blocks = lax.scan(
        attend_back,
        (zero_state, zero_state),
        (jnp.arange(block_count, dtype=jnp.int32), log_totals),
    )
    g_stack = jnp.stack(
        [
            to_owned(g_query_blocks.reshape(tok_count, local_heads * HD), groups, pieces),
            to_owned(
                grad_key.reshape(tok_count, local_heads * HD).astype(jnp.bfloat16), groups, pieces
            ),
            to_owned(
                grad_value.reshape(tok_count, local_heads * HD).astype(jnp.bfloat16), groups, pieces
            ),
        ]
    )
    scale_vec = jnp.array([query_scale, 1.0, 1.0], jnp.float32)
    grad_w_qkv = (
        jnp.einsum("td,cte->cde", dealt_owned, g_stack, preferred_element_type=jnp.float32)
        * scale_vec[:, None, None]
    )
    grad_b_qv = jnp.stack(
        [
            query_scale * jnp.sum(g_stack[0].astype(jnp.float32), axis=0),
            jnp.sum(g_stack[2].astype(jnp.float32), axis=0),
        ]
    )
    scaled_weights = wqkv_low * jnp.array([query_scale, 1.0, 1.0], jnp.bfloat16)[:, None, None]
    picked = g_stack
    g_input_proj = lax.psum_scatter(
        jnp.einsum(
            "cte,cde->td", picked, scaled_weights, preferred_element_type=jnp.float32
        ).astype(jnp.bfloat16),
        "tensor",
        scatter_dimension=0,
        tiled=True,
    ).astype(jnp.float32)
    g_input_low = (g_first + g_input_proj).astype(jnp.bfloat16)
    back_result, back_input = (
        lax.all_to_all(result.astype(jnp.bfloat16), "dp", split_axis=0, concat_axis=0, tiled=True),
        lax.all_to_all(g_input_low, "dp", split_axis=0, concat_axis=0, tiled=True),
    )
    width = back_result.shape[1]
    full_result, full_input = (
        lax.all_gather(back_result.reshape(groups, sub_len, width), "tensor", axis=1, tiled=True),
        lax.all_gather(back_input.reshape(groups, sub_len, width), "tensor", axis=1, tiled=True),
    )
    output = full_result.reshape(tok_count, width)[slot_index]
    input_grad = full_input.reshape(tok_count, width)[slot_index]
    grad_w_qkv, grad_b_qv, grad_w_out, grad_w_up, grad_b_up, grad_w_down = lax.psum(
        (grad_w_qkv, grad_b_qv, grad_w_out, grad_w_up, grad_b_up, grad_w_down), "dp"
    )
    grad_b_out, grad_ln1_gain, grad_ln1_bias, grad_b_down, grad_ln2_gain, grad_ln2_bias = lax.psum(
        (grad_b_out, grad_ln1_gain, grad_ln1_bias, grad_b_down, grad_ln2_gain, grad_ln2_bias),
        ("dp", "tensor"),
    )
    return (
        output,
        input_grad,
        grad_w_qkv,
        grad_b_qv,
        grad_w_out,
        grad_b_out,
        grad_ln1_gain,
        grad_ln1_bias,
        grad_w_up,
        grad_b_up,
        grad_w_down,
        grad_b_down,
        grad_ln2_gain,
        grad_ln2_bias,
    )


def solution(mesh):
    placed = (
        P("dp", None),
        P("dp", None),
        P("dp"),
        P(None, None, "tensor"),
        P(None, "tensor"),
        P("tensor", None),
        P(),
        P(),
        P(),
        P(None, "tensor"),
        P("tensor"),
        P("tensor", None),
        P(),
        P(),
        P(),
        P("dp", None),
    )
    return jax.shard_map(
        on_device,
        mesh=mesh,
        in_specs=placed,
        out_specs=(
            P("dp", None),
            P("dp", None),
            P(None, None, "tensor"),
            P(None, "tensor"),
            P("tensor", None),
            P(),
            P(),
            P(),
            P(None, "tensor"),
            P("tensor"),
            P("tensor", None),
            P(),
            P(),
            P(),
        ),
        check_vma=False,
    )
```

profile of v0, /device:TPU:0, one launch (start us, length us, event | category | flops | bytes accessed | tf_op | source)
XLA Modules:
  0.0 924.4 jit_solution(1465354280746860340)
XLA Ops:
  7.9 9.7 %scatter_custom_fusion = bf16[1536,768]{1,0:T(8,128)(2,1)} fusion(s32[1536]{0:T(1024)S(1)} %compare_select_fusion, bf16[1536,768]{1,0:T(8,128)(2,1)} %param.22, bf16[]{:T(256)} %constant.40.clone.1), kind=kCustom, calls=%fused_computation.93 | custom fusion | bytes 2359808 | tf_op jit(solution)/shard_map/scatter | solution.py:68
  17.6 5.3 all-to-all-start
  25.0 27.3 %all-to-all-done = bf16[8,192,768]{2,1,0:T(8,128)(2,1)S(1)} async-done(((bf16[8,192,768]{2,1,0:T(8,128)(2,1)}), bf16[8,192,768]{2,1,0:T(8,128)(2,1)S(1)}, u32[]{:S(2)}, u32[]{:S(2)}) %all-to-all-start) | async-done | bytes 2359328 | tf_op jit(solution)/shard_map/all_to_all | solution.py:71
  54.5 28.7 %while.27 = (s32[]{:T(128)}, bf16[3,512,3,64]{1,3,2,0:T(8,128)(2,1)S(1)}, f32[3,3,512]{2,1,0:T(4,128)}, s32[3]{0:T(128)S(1)}, s32[1536]{0:T(1024)S(1)}, /*index=...) while((s32[]{:T(128)}, ...), condition=%wide.region_6.7_spmd, body=%wide.region_3.6_spmd.sunk | while | flops 626096640 | bytes 33097928 | solution.py:117
  58.0 2.6 fusion.124
  60.6 2.8 fusion.125
  70.2 2.8 fusion.125
  79.8 2.8 fusion.125
  84.0 2.7 copy.48
  90.9 4.0 fusion.63
  96.7 83.0 %reduce-scatter.5.cloned.1.call-done = f32[384,768]{1,0:T(8,128)} async-done(((f32[1536,768]{1,0:T(8,128)}), f32[384,768]{1,0:T(8,128)}) %reduce-scatter.5.cloned.1.call-update) | async-done | bytes 1179664 | tf_op jit(solution)/shard_map/reduce_scatter | solution.py:121
  182.7 51.1 %all-gather.6.cloned.1.call-done = bf16[1536,768]{1,0:T(8,128)(2,1)} async-done(((bf16[384,768]{1,0:T(8,128)(2,1)}), bf16[1536,768]{1,0:T(8,128)(2,1)}) %all-gather.6.cloned.1.call-update) | async-done | bytes 2359312 | tf_op jit(solution)/shard_map/all_gather | solution.py:130
  233.8 15.6 %multiply_convert_fusion.1 = (bf16[1536,768]{1,0:T(8,128)(2,1)S(1)}, f32[1536,768]{1,0:T(8,128)}, f32[1536,768]{1,0:T(8,128)}) fusion(f32[768]{0:T(1024)S(1)} %convert_convert_fusion.1, bf16[1536,768]{1,0:T(8,128)(2,1)} %all-gather.6.cloned.1.call-done, f32[768,768]{1,0:T(8,128)} %param.31), kind=kOutput, calls=%fused_computation.51 | convolution fusion | flops 1890385920 | bytes 16518144 | tf_op jit(solution)/shard_map/dot_general | solution.py:131
  250.8 4.3 fusion.53
  255.1 9.7 %scatter_custom_fusion.1 = bf16[1536,768]{1,0:T(8,128)(2,1)} fusion(s32[1536]{0:T(1024)} %copy-done.30, bf16[1536,768]{1,0:T(8,128)(2,1)} %param.37, bf16[]{:T(256)} %constant.40.clone.1), kind=kCustom, calls=%fused_computation.91 | custom fusion | bytes 2359808 | tf_op jit(solution)/shard_map/scatter | solution.py:69
  264.8 4.5 all-to-all-start.2
  270.4 69.0 %reduce-scatter.7.cloned.1.call-done = f32[384,768]{1,0:T(8,128)} async-done(((f32[1536,768]{1,0:T(8,128)}), f32[384,768]{1,0:T(8,128)}) %reduce-scatter.7.cloned.1.call-update) | async-done | bytes 1179664 | tf_op jit(solution)/shard_map/reduce_scatter | solution.py:137
  351.2 51.1 %all-gather.10.cloned.1.call-done = bf16[1536,768]{1,0:T(8,128)(2,1)} async-done(((bf16[384,768]{1,0:T(8,128)(2,1)}), bf16[1536,768]{1,0:T(8,128)(2,1)}) %all-gather.10.cloned.1.call-update) | async-done | bytes 2359312 | tf_op jit(solution)/shard_map/all_gather | solution.py:148
  402.3 9.3 %convert_reduce_fusion = (f32[768]{0:T(1024)}, bf16[1536,768]{1,0:T(8,128)(2,1)S(1)}) fusion(f32[1536,768]{1,0:T(8,128)} %get-tuple-element.222, bf16[1536,768]{1,0:T(8,128)(2,1)} %all-gather.10.cloned.1.call-done, f32[768,768]{1,0:T(8,128)} %param.33, f32[1536,768]{1,0:T(8,128)} %get-tuple-element.236, f32[768]{0:T(1024)S(1)} %copy-done.46), kind=kOutput, calls=%fused_computation.49 | convolution fusion | flops 1832582400 | bytes 16521216 | tf_op jit(solution)/shard_map/dot_general | solution.py:149
  413.0 4.3 fusion.57
  417.3 84.2 %reduce-scatter.9.cloned.1.call-done = f32[384,768]{1,0:T(8,128)} async-done(((f32[1536,768]{1,0:T(8,128)}), f32[384,768]{1,0:T(8,128)}) %reduce-scatter.9.cloned.1.call-update) | async-done | bytes 1179664 | tf_op jit(solution)/shard_map/reduce_scatter | solution.py:155
  508.6 51.1 %all-gather.12.cloned.1.call-done = bf16[1536,768]{1,0:T(8,128)(2,1)} async-done(((bf16[384,768]{1,0:T(8,128)(2,1)}), bf16[1536,768]{1,0:T(8,128)(2,1)}) %all-gather.12.cloned.1.call-update) | async-done | bytes 2359312 | tf_op jit(solution)/shard_map/all_gather | solution.py:164
  564.2 54.1 %while.28 = (s32[]{:T(128)}, f32[1536,3,64]{0,2,1:T(8,128)S(1)}, f32[1536,3,64]{0,2,1:T(8,128)S(1)}, bf16[3,512,3,64]{1,3,2,0:T(8,128)(2,1)}, s32[3]{0:T(128)S(1...) while((s32[]{:T(128)}, f32[1536,3,64]{0,2,1:T(8,128)S(1)}, ...), condition=%wide.region_21.22_spmd.clone, body=%wide.region_19.21_spmd.clone.sunk | while | flops 1540323840 | bytes 83814672 | solution.py:198
  569.3 2.7 fusion.137
  572.0 3.4 multiply_reduce_fusion.6
  575.4 2.7 multiply_convert_fusion.4
  587.3 2.7 fusion.137
  590.0 3.4 multiply_reduce_fusion.6
  593.4 2.7 multiply_convert_fusion.4
  605.3 2.7 fusion.137
  608.0 3.4 multiply_reduce_fusion.6
  611.4 2.7 multiply_convert_fusion.4
  626.2 2.9 copy.54
  632.6 3.0 reshape_reshape.7
  636.8 5.2 bitcast_convert_fusion
  642.1 14.8 %all_to_all.39 = bf16[8,48,768]{2,1,0:T(8,128)(2,1)} all-to-all(bf16[8,48,768]{2,1,0:T(8,128)(2,1)} %bitcast.174), channel_id=1, replica_groups=mesh['dp'=8,'tensor'=4] {'dp'}, dimensions={0} | all-to-all | bytes 1179648 | tf_op jit(solution)/shard_map/all_to_all | solution.py:237
  656.9 32.1 %reduce-scatter.11.cloned.1.call-done = bf16[384,768]{1,0:T(8,128)(2,1)} async-done(((bf16[1536,768]{1,0:T(8,128)(2,1)}), bf16[384,768]{1,0:T(8,128)(2,1)}) %reduce-scatter.11.cloned.1.call-update) | async-done | bytes 589840 | tf_op jit(solution)/shard_map/reduce_scatter | solution.py:227
  690.3 14.0 %all_to_all.40 = bf16[8,48,768]{2,1,0:T(8,128)(2,1)} all-to-all(bf16[8,48,768]{2,1,0:T(8,128)(2,1)S(1)} %bitcast.173), channel_id=1, replica_groups=mesh['dp'=8,'tensor'=4] {'dp'}, dimensions={0} | all-to-all | bytes 1179648 | tf_op jit(solution)/shard_map/all_to_all | solution.py:238
  707.5 3.5 fusion.81
  711.0 3.5 fusion.80
  716.0 2.8 multiply_bitcast_fusion
  720.7 19.9 %all-gather.8.cloned.1.call-done = bf16[8,192,768]{2,1,0:T(8,128)(2,1)} async-done(((bf16[8,48,768]{2,1,0:T(8,128)(2,1)}), bf16[8,192,768]{2,1,0:T(8,128)(2,1)}) %all-gather.8.cloned.1.call-update) | async-done | bytes 2359312 | tf_op jit(solution)/shard_map/all_gather | solution.py:242
  740.6 8.7 gather_fusion
  749.3 43.3 %all-reduce = (f32[768]{0:T(1024)}, f32[768]{0:T(1024)}, f32[768]{0:T(1024)}, f32[768]{0:T(1024)}, f32[768]{0:T(1024)}, /*index=5*/f32[768]{0:T(1024)}) all-reduce(f32[768]{0:T(1024)S(1)} %copy-done.38, f32[768]{0:T(1024)S(1)} %copy-done.39, f32[768]{0:T(1024)S(1)} %copy-done.40, ...), channel_id=1, replica_groups=mesh['dp'=8,'tensor'=4] {'dp','tensor'}, use_global_device_ids=true, to_apply=%region_29.30 | all-reduce | flops 4608 | bytes 36864 | tf_op jit(solution)/shard_map/psum | solution.py:250
  794.3 14.2 %all-reduce.1 = (f32[2,192]{1,0:T(2,128)}, f32[768]{0:T(1024)}) all-reduce(f32[2,192]{1,0:T(2,128)S(1)} %pad_maximum_fusion.3, f32[768]{0:T(1024)S(1)} %copy-done.41), channel_id=1, replica_groups=mesh['dp'=8,'tensor'=4] {'dp'}, use_global_device_ids=true, to_apply=%region_26.27 | all-reduce | flops 1152 | bytes 9216 | tf_op jit(solution)/shard_map/psum | solution.py:247
  808.5 8.7 gather_fusion.1
  817.2 92.3 %all-reduce.5.cloned.1.call-done = (f32[3,768,192]{1,2,0:T(8,128)}, f32[192,768]{1,0:T(8,128)}, f32[768,768]{1,0:T(8,128)}, f32[768,768]{1,0:T(8,128)}) async-done(((f32[3,768,192]{1,2,0:T(8,128)}, f32[192,768]{1,0:T(8,128)}, f32[768,768]{1,0:T(8,128)}, f32[768,768]{1,0:T(8,128)}), (f32[3,768,192]{1,2,0:T(8,128)}, f32[192,768]{1,0:T(8,128)}, f32[768,768]{1,0:T(8,128)}, ...) | async-done | bytes 7077904 | tf_op jit(solution)/shard_map/psum | solution.py:247
  909.5 2.9 copy.92
  (238 shorter events, 109.7 us)
Async XLA Ops:
  7.9 9.7 %copy-start.30 = (s32[1536]{0:T(1024)}, s32[1536]{0:T(1024)S(1)}, u32[]{:S(2)}) copy-start(s32[1536]{0:T(1024)S(1)} %compare_select_fusion) | copy-start | bytes 18436
  17.6 5.4 copy-start.50
  17.6 5.6 copy-start.47
  17.6 34.8 %all-to-all-start = ((bf16[8,192,768]{2,1,0:T(8,128)(2,1)}), bf16[8,192,768]{2,1,0:T(8,128)(2,1)S(1)}, u32[]{:S(2)}, u32[]{:S(2)}) async-start(bf16[8,192,768]{2,1,0:T(8,128)(2,1)} %bitcast.158), calls=%async_computation | async-start | bytes 4718592 | tf_op jit(solution)/shard_map/all_to_all | solution.py:71
  22.9 156.8 %reduce-scatter.5.cloned.1.call-start = ((), (), s32[]{:S(2)}) async-start(), calls=%async_computation.8 | async-start | bytes 5898240 | tf_op jit(solution)/shard_map/reduce_scatter | solution.py:121
  24.9 29.0 %copy-start.22 = (bf16[3,768,192]{1,2,0:T(8,128)(2,1)}, bf16[3,768,192]{1,2,0:T(8,128)(2,1)S(1)}, u32[]{:S(2)}) copy-start(bf16[3,768,192]{1,2,0:T(8,128)(2,1)S(1)} %convert_element_type.144) | copy-start | bytes 2654212
  84.0 6.0 copy-start
  94.9 138.9 %all-gather.6.cloned.1.call-start = ((), (), s32[]{:S(2)}) async-start(), calls=%async_computation.9 | async-start | bytes 2949120 | tf_op jit(solution)/shard_map/all_gather | solution.py:130
  96.6 84.9 %copy-start.27 = (f32[768]{0:T(1024)S(1)}, f32[768]{0:T(1024)}, u32[]{:S(2)}) copy-start(f32[768]{0:T(1024)} %param.29) | copy-start | bytes 9220
  96.6 84.9 %copy-start.35 = (f32[768]{0:T(1024)S(1)}, f32[768]{0:T(1024)}, u32[]{:S(2)}) copy-start(f32[768]{0:T(1024)} %param.30) | copy-start | bytes 9220
  181.5 67.9 %copy-start.32 = (f32[384]{0:T(512)}, f32[384]{0:T(512)S(1)}, u32[]{:S(2)}) copy-start(f32[384]{0:T(512)S(1)} %multiply_reduce_fusion.4) | copy-start | bytes 4612
  181.5 67.9 %copy-start.28 = (f32[384]{0:T(512)}, f32[384]{0:T(512)S(1)}, u32[]{:S(2)}) copy-start(f32[384]{0:T(512)S(1)} %fusion.68) | copy-start | bytes 4612
  182.6 156.7 %reduce-scatter.7.cloned.1.call-start = ((), (), s32[]{:S(2)}) async-start(), calls=%async_computation.10 | async-start | bytes 5898240 | tf_op jit(solution)/shard_map/reduce_scatter | solution.py:137
  182.7 66.7 %copy-start.45 = (f32[768]{0:T(1024)}, f32[768]{0:T(1024)S(1)}, u32[]{:S(2)}) copy-start(f32[768]{0:T(1024)S(1)} %convert_convert_fusion.1) | copy-start | bytes 9220
  233.8 17.0 %copy-start.48 = (f32[768,768]{1,0:T(8,128)S(1)}, f32[768,768]{1,0:T(8,128)}, u32[]{:S(2)}) copy-start(f32[768,768]{1,0:T(8,128)} %param.33) | copy-start | bytes 7077892
  264.8 5.0 copy-start.44
  264.8 78.3 %all-to-all-start.2 = ((bf16[8,192,768]{2,1,0:T(8,128)(2,1)}), bf16[8,192,768]{2,1,0:T(8,128)(2,1)}, u32[]{:S(2)}, u32[]{:S(2)}) async-start(bf16[8,192,768]{2,1,0:T(8,128)(2,1)} %bitcast.159), calls=%async_computation.4 | async-start | bytes 4718592 | tf_op jit(solution)/shard_map/all_to_all | solution.py:72
  269.3 133.0 %all-gather.10.cloned.1.call-start = ((), (), s32[]{:S(2)}) async-start(), calls=%async_computation.12 | async-start | bytes 2949120 | tf_op jit(solution)/shard_map/all_gather | solution.py:148
  348.5 53.8 %copy-start.46 = (f32[768]{0:T(1024)S(1)}, f32[768]{0:T(1024)}, u32[]{:S(2)}) copy-start(f32[768]{0:T(1024)} %copy-done.45) | copy-start | bytes 9220
  348.5 63.1 %copy-start.34 = (f32[384]{0:T(512)}, f32[384]{0:T(512)S(1)}, u32[]{:S(2)}) copy-start(f32[384]{0:T(512)S(1)} %negate_multiply_fusion.2) | copy-start | bytes 4612
  351.1 150.4 %reduce-scatter.9.cloned.1.call-start = ((), (), s32[]{:S(2)}) async-start(), calls=%async_computation.13 | async-start | bytes 5898240 | tf_op jit(solution)/shard_map/reduce_scatter | solution.py:155
  402.3 10.7 %copy-start.49 = (f32[768,768]{1,0:T(8,128)S(1)}, f32[768,768]{1,0:T(8,128)}, u32[]{:S(2)}) copy-start(f32[768,768]{1,0:T(8,128)} %param.31) | copy-start | bytes 7077892
  417.2 84.3 %copy-start.6 = (f32[384,768]{1,0:T(8,128)S(1)}, f32[384,768]{1,0:T(8,128)}, u32[]{:S(2)}) copy-start(f32[384,768]{1,0:T(8,128)} %copy-done.5) | copy-start | bytes 3538948
  417.3 142.4 %all-gather.12.cloned.1.call-start = ((), (), s32[]{:S(2)}) async-start(), calls=%async_computation.14 | async-start | bytes 2949120 | tf_op jit(solution)/shard_map/all_gather | solution.py:164
  508.5 180.5 %reduce-scatter.11.cloned.1.call-start = ((), (), s32[]{:S(2)}) async-start(), calls=%async_computation.15 | async-start | bytes 2949120 | tf_op jit(solution)/shard_map/reduce_scatter | solution.py:227
  566.9 2.4 copy-start.1
  602.8 2.4 copy-start.1
  620.9 2.9 copy-start.19
  626.2 4.0 copy-start.20
  632.6 4.2 copy-start.52
  642.0 47.0 %copy-start.4 = (f32[384,768]{1,0:T(8,128)S(1)}, f32[384,768]{1,0:T(8,128)}, u32[]{:S(2)}) copy-start(f32[384,768]{1,0:T(8,128)} %copy-done.3) | copy-start | bytes 3538948
  642.0 98.5 %all-gather.8.cloned.1.call-start = ((), (), s32[]{:S(2)}) async-start(), calls=%async_computation.11 | async-start | bytes 2949120 | tf_op jit(solution)/shard_map/all_gather | solution.py:242
  656.8 151.7 %all-gather.14.cloned.1.call-start = ((), (), s32[]{:S(2)}) async-start(), calls=%async_computation.16 | async-start | bytes 2949120 | tf_op jit(solution)/shard_map/all_gather | solution.py:243
  704.3 205.1 %all-reduce.5.cloned.1.call-start = ((), (), s32[]{:S(2)}) async-start(), calls=%async_computation.17 | async-start | bytes 14155776 | tf_op jit(solution)/shard_map/psum | solution.py:247
  704.4 3.1 copy-start.14
  707.5 3.5 copy-start.11
  707.5 3.5 copy-start.16
  711.0 3.5 copy-start.7
  711.0 3.5 copy-start.9
  740.5 8.7 copy-start.36
  740.5 8.7 copy-start.37
  740.5 8.7 copy-start.38
  740.6 8.7 copy-start.39
  740.6 8.8 copy-start.40
  749.3 45.0 %copy-start.41 = (f32[768]{0:T(1024)S(1)}, f32[768]{0:T(1024)}, u32[]{:S(2)}) copy-start(f32[768]{0:T(1024)} %get-tuple-element.237) | copy-start | bytes 9220
  909.5 3.0 copy-start.23
  909.5 3.8 copy-start.18
  913.2 2.5 copy-start.17
  (19 other events, 24.9 us)
Sparse Core Ops, SparseCore 0:
  95.0 84.6 reduce-scatter.4
  182.8 50.9 all-gather.5
  255.2 84.0 reduce-scatter.6
  351.2 50.9 all-gather.9
  417.4 84.0 reduce-scatter.8
  508.6 50.9 all-gather.11
  642.1 46.8 reduce-scatter.10
  690.6 49.9 all-gather.7
  742.1 50.2 all-gather.13
  797.1 112.2 all-reduce.4
where the time goes:
time: 934 us; the launch traced here: 924 us
  waiting for transfers between devices  561 us (60%)
  matrix products  109 us (12%)
  local copies, waits for them, and re-layouts  90.2 us (10%)
  blocking collectives  86.4 us (9%)
  other arithmetic  47.6 us (5%)
  between operations  15.2 us (2%)
  starting transfers between devices  10.8 us (1%)
    psum x1, waiting for transfers between devices, on_device(): lax.psum((grad_w_qkv, grad_b_qv, grad_w_out, grad_w_up, grad_b_up, grad_w...  92.3 us
    reduce_scatter x1, waiting for transfers between devices, on_device(): lax.psum_scatter(jnp.dot(picked, wup_low.T, preferred_element_type=jnp.fl...  84.2 us
    reduce_scatter x1, waiting for transfers between devices, on_device(): lax.psum_scatter(jnp.dot(picked, wout_low, preferred_element_type=jnp.flo...  83 us
    reduce_scatter x1, waiting for transfers between devices, on_device(): lax.psum_scatter(jnp.dot(picked, wdown_low, preferred_element_type=jnp.fl...  69 us
    all_gather x1, waiting for transfers between devices, on_device(): g_ffn_all = lax.all_gather(g_ffn_low, 'tensor', axis=0, tiled=True)  51.1 us
    all_gather x1, waiting for transfers between devices, on_device(): lax.all_gather(g_first.astype(jnp.bfloat16), 'tensor', axis=0, tiled=True)  51.1 us
    all_gather x1, waiting for transfers between devices, on_device(): hidden_all = lax.all_gather(hidden_low, 'tensor', axis=0, tiled=True)  51.1 us
    psum x1, blocking collectives, on_device(): lax.psum((grad_b_out, grad_ln1_gain, grad_ln1_bias, grad_b_down, grad_ln2...  43.3 us
  transfers between devices with their start and end apart: 12, of which 10 were waited for; matrix products, arithmetic and copies ran while one was open for 5% of the time, Pallas kernels for 0%

commit v1 on v0

--- a/solution.py
+++ b/solution.py
@@ -248,8 +248,11 @@
         (grad_w_qkv, grad_b_qv, grad_w_out, grad_w_up, grad_b_up, grad_w_down), "dp"
     )
     grad_b_out, grad_ln1_gain, grad_ln1_bias, grad_b_down, grad_ln2_gain, grad_ln2_bias = lax.psum(
-        (grad_b_out, grad_ln1_gain, grad_ln1_bias, grad_b_down, grad_ln2_gain, grad_ln2_bias),
-        ("dp", "tensor"),
+        lax.psum(
+            (grad_b_out, grad_ln1_gain, grad_ln1_bias, grad_b_down, grad_ln2_gain, grad_ln2_bias),
+            "tensor",
+        ),
+        "dp",
     )
     return (
         output,

time: 934 us -> 934 us (level)
  blocking collectives: 86.4 us -> 71.3 us
  waiting for transfers between devices: 561 us -> 576 us
    psum x1, blocking collectives: 43.3 us -> 17.9 us  [on_device(): lax.psum((grad_b_out, grad_ln1_gain, grad_ln1_bias, grad_b_down, grad_ln2...]
    psum x1, waiting for transfers between devices: 92.3 us -> 107 us  [on_device(): lax.psum((grad_w_qkv, grad_b_qv, grad_w_out, grad_w_up, grad_b_up, grad_w...]
    psum x1, blocking collectives: 14.2 us -> 24.6 us  [on_device(): lax.psum((grad_w_qkv, grad_b_qv, grad_w_out, grad_w_up, grad_b_up, grad_w...]
where the time goes in v1:
time: 934 us; the launch traced here: 924 us
  waiting for transfers between devices  576 us (62%)
  matrix products  109 us (12%)
  local copies, waits for them, and re-layouts  90.2 us (10%)
  blocking collectives  71.3 us (8%)
  other arithmetic  47.6 us (5%)
  between operations  15.2 us (2%)
  starting transfers between devices  10.8 us (1%)
    psum x1, waiting for transfers between devices, on_device(): lax.psum((grad_w_qkv, grad_b_qv, grad_w_out, grad_w_up, grad_b_up, grad_w...  107 us
    reduce_scatter x1, waiting for transfers between devices, on_device(): lax.psum_scatter(jnp.dot(picked, wup_low.T, preferred_element_type=jnp.fl...  84.2 us
    reduce_scatter x1, waiting for transfers between devices, on_device(): lax.psum_scatter(jnp.dot(picked, wout_low, preferred_element_type=jnp.flo...  83 us
    reduce_scatter x1, waiting for transfers between devices, on_device(): lax.psum_scatter(jnp.dot(picked, wdown_low, preferred_element_type=jnp.fl...  69 us
    all_gather x1, waiting for transfers between devices, on_device(): g_ffn_all = lax.all_gather(g_ffn_low, 'tensor', axis=0, tiled=True)  51.1 us
    all_gather x1, waiting for transfers between devices, on_device(): lax.all_gather(g_first.astype(jnp.bfloat16), 'tensor', axis=0, tiled=True)  51.1 us
    all_gather x1, waiting for transfers between devices, on_device(): hidden_all = lax.all_gather(hidden_low, 'tensor', axis=0, tiled=True)  51.1 us
    reduce_scatter x1, waiting for transfers between devices, on_device(): lax.psum_scatter(jnp.einsum('cte,cde->td', picked, scaled_weights, prefer...  32.1 us
  transfers between devices with their start and end apart: 12, of which 10 were waited for; matrix products, arithmetic and copies ran while one was open for 5% of the time, Pallas kernels for 0%

profile of v1, /device:TPU:0, one launch (start us, length us, event | category | flops | bytes accessed | tf_op | source)
XLA Modules:
  0.0 924.3 jit_solution(15093602903755511020)
XLA Ops:
  7.9 9.7 %scatter_custom_fusion = bf16[1536,768]{1,0:T(8,128)(2,1)} fusion(s32[1536]{0:T(1024)S(1)} %compare_select_fusion, bf16[1536,768]{1,0:T(8,128)(2,1)} %param.22, bf16[]{:T(256)} %constant.40.clone.1), kind=kCustom, calls=%fused_computation.93 | custom fusion | bytes 2359808 | tf_op jit(solution)/shard_map/scatter | solution.py:68
  17.6 5.3 all-to-all-start
  25.0 27.3 %all-to-all-done = bf16[8,192,768]{2,1,0:T(8,128)(2,1)S(1)} async-done(((bf16[8,192,768]{2,1,0:T(8,128)(2,1)}), bf16[8,192,768]{2,1,0:T(8,128)(2,1)S(1)}, u32[]{:S(2)}, u32[]{:S(2)}) %all-to-all-start) | async-done | bytes 2359328 | tf_op jit(solution)/shard_map/all_to_all | solution.py:71
  54.5 28.7 %while.27 = (s32[]{:T(128)}, bf16[3,512,3,64]{1,3,2,0:T(8,128)(2,1)S(1)}, f32[3,3,512]{2,1,0:T(4,128)}, s32[3]{0:T(128)S(1)}, s32[1536]{0:T(1024)S(1)}, /*index=...) while((s32[]{:T(128)}, ...), condition=%wide.region_6.7_spmd, body=%wide.region_3.6_spmd.sunk | while | flops 626096640 | bytes 33097928 | solution.py:117
  58.0 2.6 fusion.124
  60.6 2.8 fusion.125
  70.2 2.8 fusion.125
  79.8 2.8 fusion.125
  84.0 2.7 copy.48
  90.9 4.0 fusion.63
  96.7 83.0 %reduce-scatter.5.cloned.1.call-done = f32[384,768]{1,0:T(8,128)} async-done(((f32[1536,768]{1,0:T(8,128)}), f32[384,768]{1,0:T(8,128)}) %reduce-scatter.5.cloned.1.call-update) | async-done | bytes 1179664 | tf_op jit(solution)/shard_map/reduce_scatter | solution.py:121
  182.7 51.1 %all-gather.6.cloned.1.call-done = bf16[1536,768]{1,0:T(8,128)(2,1)} async-done(((bf16[384,768]{1,0:T(8,128)(2,1)}), bf16[1536,768]{1,0:T(8,128)(2,1)}) %all-gather.6.cloned.1.call-update) | async-done | bytes 2359312 | tf_op jit(solution)/shard_map/all_gather | solution.py:130
  233.8 15.6 %multiply_convert_fusion.1 = (bf16[1536,768]{1,0:T(8,128)(2,1)S(1)}, f32[1536,768]{1,0:T(8,128)}, f32[1536,768]{1,0:T(8,128)}) fusion(f32[768]{0:T(1024)S(1)} %convert_convert_fusion.1, bf16[1536,768]{1,0:T(8,128)(2,1)} %all-gather.6.cloned.1.call-done, f32[768,768]{1,0:T(8,128)} %param.31), kind=kOutput, calls=%fused_computation.51 | convolution fusion | flops 1890385920 | bytes 16518144 | tf_op jit(solution)/shard_map/dot_general | solution.py:131
  250.8 4.3 fusion.53
  255.1 9.7 %scatter_custom_fusion.1 = bf16[1536,768]{1,0:T(8,128)(2,1)} fusion(s32[1536]{0:T(1024)} %copy-done.30, bf16[1536,768]{1,0:T(8,128)(2,1)} %param.37, bf16[]{:T(256)} %constant.40.clone.1), kind=kCustom, calls=%fused_computation.91 | custom fusion | bytes 2359808 | tf_op jit(solution)/shard_map/scatter | solution.py:69
  264.8 4.5 all-to-all-start.2
  270.4 69.0 %reduce-scatter.7.cloned.1.call-done = f32[384,768]{1,0:T(8,128)} async-done(((f32[1536,768]{1,0:T(8,128)}), f32[384,768]{1,0:T(8,128)}) %reduce-scatter.7.cloned.1.call-update) | async-done | bytes 1179664 | tf_op jit(solution)/shard_map/reduce_scatter | solution.py:137
  351.2 51.1 %all-gather.10.cloned.1.call-done = bf16[1536,768]{1,0:T(8,128)(2,1)} async-done(((bf16[384,768]{1,0:T(8,128)(2,1)}), bf16[1536,768]{1,0:T(8,128)(2,1)}) %all-gather.10.cloned.1.call-update) | async-done | bytes 2359312 | tf_op jit(solution)/shard_map/all_gather | solution.py:148
  402.3 9.3 %convert_reduce_fusion = (f32[768]{0:T(1024)}, bf16[1536,768]{1,0:T(8,128)(2,1)S(1)}) fusion(f32[1536,768]{1,0:T(8,128)} %get-tuple-element.228, bf16[1536,768]{1,0:T(8,128)(2,1)} %all-gather.10.cloned.1.call-done, f32[768,768]{1,0:T(8,128)} %param.33, f32[1536,768]{1,0:T(8,128)} %get-tuple-element.242, f32[768]{0:T(1024)S(1)} %copy-done.46), kind=kOutput, calls=%fused_computation.49 | convolution fusion | flops 1832582400 | bytes 16521216 | tf_op jit(solution)/shard_map/dot_general | solution.py:149
  413.0 4.3 fusion.57
  417.3 84.2 %reduce-scatter.9.cloned.1.call-done = f32[384,768]{1,0:T(8,128)} async-done(((f32[1536,768]{1,0:T(8,128)}), f32[384,768]{1,0:T(8,128)}) %reduce-scatter.9.cloned.1.call-update) | async-done | bytes 1179664 | tf_op jit(solution)/shard_map/reduce_scatter | solution.py:155
  508.6 51.1 %all-gather.12.cloned.1.call-done = bf16[1536,768]{1,0:T(8,128)(2,1)} async-done(((bf16[384,768]{1,0:T(8,128)(2,1)}), bf16[1536,768]{1,0:T(8,128)(2,1)}) %all-gather.12.cloned.1.call-update) | async-done | bytes 2359312 | tf_op jit(solution)/shard_map/all_gather | solution.py:164
  564.2 54.1 %while.28 = (s32[]{:T(128)}, f32[1536,3,64]{0,2,1:T(8,128)S(1)}, f32[1536,3,64]{0,2,1:T(8,128)S(1)}, bf16[3,512,3,64]{1,3,2,0:T(8,128)(2,1)}, s32[3]{0:T(128)S(1...) while((s32[]{:T(128)}, f32[1536,3,64]{0,2,1:T(8,128)S(1)}, ...), condition=%wide.region_21.22_spmd.clone, body=%wide.region_19.21_spmd.clone.sunk | while | flops 1540323840 | bytes 83814672 | solution.py:198
  569.3 2.7 fusion.137
  572.0 3.4 multiply_reduce_fusion.6
  575.4 2.7 multiply_convert_fusion.4
  587.3 2.7 fusion.137
  590.0 3.4 multiply_reduce_fusion.6
  593.4 2.7 multiply_convert_fusion.4
  605.3 2.7 fusion.137
  608.0 3.4 multiply_reduce_fusion.6
  611.4 2.7 multiply_convert_fusion.4
  626.2 2.9 copy.54
  632.6 3.0 reshape_reshape.7
  636.8 5.2 bitcast_convert_fusion
  642.1 14.8 %all_to_all.39 = bf16[8,48,768]{2,1,0:T(8,128)(2,1)} all-to-all(bf16[8,48,768]{2,1,0:T(8,128)(2,1)} %bitcast.174), channel_id=1, replica_groups=mesh['dp'=8,'tensor'=4] {'dp'}, dimensions={0} | all-to-all | bytes 1179648 | tf_op jit(solution)/shard_map/all_to_all | solution.py:237
  656.9 32.1 %reduce-scatter.11.cloned.1.call-done = bf16[384,768]{1,0:T(8,128)(2,1)} async-done(((bf16[1536,768]{1,0:T(8,128)(2,1)}), bf16[384,768]{1,0:T(8,128)(2,1)}) %reduce-scatter.11.cloned.1.call-update) | async-done | bytes 589840 | tf_op jit(solution)/shard_map/reduce_scatter | solution.py:227
  690.3 14.0 %all_to_all.40 = bf16[8,48,768]{2,1,0:T(8,128)(2,1)} all-to-all(bf16[8,48,768]{2,1,0:T(8,128)(2,1)S(1)} %bitcast.173), channel_id=1, replica_groups=mesh['dp'=8,'tensor'=4] {'dp'}, dimensions={0} | all-to-all | bytes 1179648 | tf_op jit(solution)/shard_map/all_to_all | solution.py:238
  707.5 3.5 fusion.81
  711.0 3.5 fusion.80
  716.0 2.8 multiply_bitcast_fusion
  720.7 19.9 %all-gather.8.cloned.1.call-done = bf16[8,192,768]{2,1,0:T(8,128)(2,1)} async-done(((bf16[8,48,768]{2,1,0:T(8,128)(2,1)}), bf16[8,192,768]{2,1,0:T(8,128)(2,1)}) %all-gather.8.cloned.1.call-update) | async-done | bytes 2359312 | tf_op jit(solution)/shard_map/all_gather | solution.py:242
  740.6 8.7 gather_fusion
  749.3 17.9 %all-reduce.2 = (f32[768]{0:T(1024)S(1)}, f32[768]{0:T(1024)S(1)}, f32[768]{0:T(1024)S(1)}, f32[768]{0:T(1024)S(1)}, f32[768]{0:T(1024)S(1)}, /*index=5*/f32[768]{0:T(1024)S(1)}) all-reduce(f32[768]{0:T(1024)S(1)} %copy-done.38, f32[768]{0:T(1024)S(1)} %copy-done.39, ...), channel_id=1, replica_groups=mesh['dp'=8,'tensor'=4] {'tensor'}, use_global_device_ids=true, to_apply=%region_29.30 | all-reduce | flops 4608 | bytes 36864 | tf_op jit(solution)/shard_map/psum | solution.py:251
  768.8 24.6 %all-reduce = (f32[2,192]{1,0:T(2,128)}, f32[768]{0:T(1024)}, f32[768]{0:T(1024)}, f32[768]{0:T(1024)}, f32[768]{0:T(1024)}, /*index=5*/f32[768]{0:T(1024)}, f32[768]{0:T(1024)}, f32[768]{0:T(1024)}) all-reduce(f32[2,192]{1,0:T(2,128)S(1)} %pad_maximum_fusion.3, ...), channel_id=1, replica_groups=mesh['dp'=8,'tensor'=4] {'dp'}, use_global_device_ids=true, to_apply=%region_26.27 | all-reduce | flops 5760 | bytes 46080 | tf_op jit(solution)/shard_map/psum | solution.py:247
  793.4 8.7 gather_fusion.1
  802.1 107.2 %all-reduce.5.cloned.1.call-done = (f32[3,768,192]{1,2,0:T(8,128)}, f32[192,768]{1,0:T(8,128)}, f32[768,768]{1,0:T(8,128)}, f32[768,768]{1,0:T(8,128)}) async-done(((f32[3,768,192]{1,2,0:T(8,128)}, f32[192,768]{1,0:T(8,128)}, f32[768,768]{1,0:T(8,128)}, f32[768,768]{1,0:T(8,128)}), (f32[3,768,192]{1,2,0:T(8,128)}, f32[192,768]{1,0:T(8,128)}, f32[768,768]{1,0:T(8,128)}, ...) | async-done | bytes 7077904 | tf_op jit(solution)/shard_map/psum | solution.py:247
  909.3 2.9 copy.92
  (238 shorter events, 109.7 us)
Async XLA Ops:
  7.9 9.7 %copy-start.30 = (s32[1536]{0:T(1024)}, s32[1536]{0:T(1024)S(1)}, u32[]{:S(2)}) copy-start(s32[1536]{0:T(1024)S(1)} %compare_select_fusion) | copy-start | bytes 18436
  17.6 5.4 copy-start.50
  17.6 5.6 copy-start.47
  17.6 34.8 %all-to-all-start = ((bf16[8,192,768]{2,1,0:T(8,128)(2,1)}), bf16[8,192,768]{2,1,0:T(8,128)(2,1)S(1)}, u32[]{:S(2)}, u32[]{:S(2)}) async-start(bf16[8,192,768]{2,1,0:T(8,128)(2,1)} %bitcast.158), calls=%async_computation | async-start | bytes 4718592 | tf_op jit(solution)/shard_map/all_to_all | solution.py:71
  22.9 156.8 %reduce-scatter.5.cloned.1.call-start = ((), (), s32[]{:S(2)}) async-start(), calls=%async_computation.8 | async-start | bytes 5898240 | tf_op jit(solution)/shard_map/reduce_scatter | solution.py:121
  24.9 29.0 %copy-start.22 = (bf16[3,768,192]{1,2,0:T(8,128)(2,1)}, bf16[3,768,192]{1,2,0:T(8,128)(2,1)S(1)}, u32[]{:S(2)}) copy-start(bf16[3,768,192]{1,2,0:T(8,128)(2,1)S(1)} %convert_element_type.144) | copy-start | bytes 2654212
  84.0 6.0 copy-start
  94.9 138.9 %all-gather.6.cloned.1.call-start = ((), (), s32[]{:S(2)}) async-start(), calls=%async_computation.9 | async-start | bytes 2949120 | tf_op jit(solution)/shard_map/all_gather | solution.py:130
  96.6 84.9 %copy-start.27 = (f32[768]{0:T(1024)S(1)}, f32[768]{0:T(1024)}, u32[]{:S(2)}) copy-start(f32[768]{0:T(1024)} %param.29) | copy-start | bytes 9220
  96.6 84.9 %copy-start.35 = (f32[768]{0:T(1024)S(1)}, f32[768]{0:T(1024)}, u32[]{:S(2)}) copy-start(f32[768]{0:T(1024)} %param.30) | copy-start | bytes 9220
  181.5 67.9 %copy-start.32 = (f32[384]{0:T(512)}, f32[384]{0:T(512)S(1)}, u32[]{:S(2)}) copy-start(f32[384]{0:T(512)S(1)} %multiply_reduce_fusion.4) | copy-start | bytes 4612
  181.5 67.9 %copy-start.28 = (f32[384]{0:T(512)}, f32[384]{0:T(512)S(1)}, u32[]{:S(2)}) copy-start(f32[384]{0:T(512)S(1)} %fusion.68) | copy-start | bytes 4612
  182.6 156.7 %reduce-scatter.7.cloned.1.call-start = ((), (), s32[]{:S(2)}) async-start(), calls=%async_computation.10 | async-start | bytes 5898240 | tf_op jit(solution)/shard_map/reduce_scatter | solution.py:137
  182.7 66.7 %copy-start.45 = (f32[768]{0:T(1024)}, f32[768]{0:T(1024)S(1)}, u32[]{:S(2)}) copy-start(f32[768]{0:T(1024)S(1)} %convert_convert_fusion.1) | copy-start | bytes 9220
  233.8 17.0 %copy-start.48 = (f32[768,768]{1,0:T(8,128)S(1)}, f32[768,768]{1,0:T(8,128)}, u32[]{:S(2)}) copy-start(f32[768,768]{1,0:T(8,128)} %param.33) | copy-start | bytes 7077892
  264.8 5.0 copy-start.44
  264.8 78.3 %all-to-all-start.2 = ((bf16[8,192,768]{2,1,0:T(8,128)(2,1)}), bf16[8,192,768]{2,1,0:T(8,128)(2,1)}, u32[]{:S(2)}, u32[]{:S(2)}) async-start(bf16[8,192,768]{2,1,0:T(8,128)(2,1)} %bitcast.159), calls=%async_computation.4 | async-start | bytes 4718592 | tf_op jit(solution)/shard_map/all_to_all | solution.py:72
  269.3 133.0 %all-gather.10.cloned.1.call-start = ((), (), s32[]{:S(2)}) async-start(), calls=%async_computation.12 | async-start | bytes 2949120 | tf_op jit(solution)/shard_map/all_gather | solution.py:148
  348.5 53.8 %copy-start.46 = (f32[768]{0:T(1024)S(1)}, f32[768]{0:T(1024)}, u32[]{:S(2)}) copy-start(f32[768]{0:T(1024)} %copy-done.45) | copy-start | bytes 9220
  348.5 63.1 %copy-start.34 = (f32[384]{0:T(512)}, f32[384]{0:T(512)S(1)}, u32[]{:S(2)}) copy-start(f32[384]{0:T(512)S(1)} %negate_multiply_fusion.2) | copy-start | bytes 4612
  351.1 150.4 %reduce-scatter.9.cloned.1.call-start = ((), (), s32[]{:S(2)}) async-start(), calls=%async_computation.13 | async-start | bytes 5898240 | tf_op jit(solution)/shard_map/reduce_scatter | solution.py:155
  402.3 10.7 %copy-start.49 = (f32[768,768]{1,0:T(8,128)S(1)}, f32[768,768]{1,0:T(8,128)}, u32[]{:S(2)}) copy-start(f32[768,768]{1,0:T(8,128)} %param.31) | copy-start | bytes 7077892
  417.2 84.3 %copy-start.6 = (f32[384,768]{1,0:T(8,128)S(1)}, f32[384,768]{1,0:T(8,128)}, u32[]{:S(2)}) copy-start(f32[384,768]{1,0:T(8,128)} %copy-done.5) | copy-start | bytes 3538948
  417.3 142.4 %all-gather.12.cloned.1.call-start = ((), (), s32[]{:S(2)}) async-start(), calls=%async_computation.14 | async-start | bytes 2949120 | tf_op jit(solution)/shard_map/all_gather | solution.py:164
  508.5 180.5 %reduce-scatter.11.cloned.1.call-start = ((), (), s32[]{:S(2)}) async-start(), calls=%async_computation.15 | async-start | bytes 2949120 | tf_op jit(solution)/shard_map/reduce_scatter | solution.py:227
  566.9 2.4 copy-start.1
  602.8 2.4 copy-start.1
  620.9 2.9 copy-start.19
  626.2 4.0 copy-start.20
  632.6 4.2 copy-start.52
  642.0 47.0 %copy-start.4 = (f32[384,768]{1,0:T(8,128)S(1)}, f32[384,768]{1,0:T(8,128)}, u32[]{:S(2)}) copy-start(f32[384,768]{1,0:T(8,128)} %copy-done.3) | copy-start | bytes 3538948
  642.0 98.5 %all-gather.8.cloned.1.call-start = ((), (), s32[]{:S(2)}) async-start(), calls=%async_computation.11 | async-start | bytes 2949120 | tf_op jit(solution)/shard_map/all_gather | solution.py:242
  656.8 136.6 %all-gather.14.cloned.1.call-start = ((), (), s32[]{:S(2)}) async-start(), calls=%async_computation.16 | async-start | bytes 2949120 | tf_op jit(solution)/shard_map/all_gather | solution.py:243
  704.3 205.0 %all-reduce.5.cloned.1.call-start = ((), (), s32[]{:S(2)}) async-start(), calls=%async_computation.17 | async-start | bytes 14155776 | tf_op jit(solution)/shard_map/psum | solution.py:247
  704.4 3.1 copy-start.14
  707.5 3.5 copy-start.11
  707.5 3.5 copy-start.16
  711.0 3.5 copy-start.7
  711.0 3.5 copy-start.9
  740.5 8.7 copy-start.36
  740.5 8.7 copy-start.37
  740.5 8.7 copy-start.38
  740.6 8.7 copy-start.39
  740.6 8.8 copy-start.40
  749.3 19.5 %copy-start.41 = (f32[768]{0:T(1024)S(1)}, f32[768]{0:T(1024)}, u32[]{:S(2)}) copy-start(f32[768]{0:T(1024)} %get-tuple-element.243) | copy-start | bytes 9220
  909.3 3.0 copy-start.23
  909.3 3.8 copy-start.18
  913.1 2.5 copy-start.17
  (19 other events, 24.9 us)
Sparse Core Ops, SparseCore 0:
  95.0 84.6 reduce-scatter.4
  182.8 50.9 all-gather.5
  255.2 84.0 reduce-scatter.6
  351.2 50.9 all-gather.9
  417.4 84.0 reduce-scatter.8
  508.6 50.9 all-gather.11
  642.1 46.8 reduce-scatter.10
  690.6 49.9 all-gather.7
  742.1 50.2 all-gather.13
  797.0 112.2 all-reduce.4
